TPU v7x, 32 devices: a whole 2x2x4 slice. The times are simulated.
32 devices in a mesh: grp: 4 (over y, x), dev: 8 (over z, core).
Axes of the slice: x: 2, y: 2, z: 4, core: 2. Of those that a mesh axis runs over, the one named last changes fastest.
Arguments:
- reach: bfloat16 [128, 64, 1326], P(('grp', 'dev')), may hold values from 0.00029945374 to 0.0029907227
- stake: float32 [128], replicated, may hold values from 1 to 10
- hand_rank: int32 [64, 1326], P(('grp', 'dev')), may hold values from 0 to 7461
- hand_live: int32 [64, 1326], P(('grp', 'dev')), may hold values 0 or 1
- board_seqs: int32 [64], P(('grp', 'dev')), may hold values from 1 to 128, 4096 in all
- board_turn: int32 [64, 1], replicated, may hold values from 0 to 15
- seq_parent: int32 [128], replicated, may hold values from 0 to 31, never falling along the last dimension, each value on 1 to 8 neighbouring positions
- set_parent: int32 [32], replicated, may hold values from 0 to 7, never falling along the last dimension, each value on 1 to 8 neighbouring positions
Outputs:
- river_values: float32 [32, 64, 1326], P(None, ('grp', 'dev'))
- turn_values: float32 [8, 16, 1326], replicated
Inputs may be any that keep to these rules, and one draw needn't show every extreme that they name: `seq_parent`: Non-decreasing; every value occurs, at most 8 times, exactly 8 times for some value. `set_parent`: Non-decreasing; every value occurs, at most 8 times, exactly 8 times for some value. `board_seqs`: some board has all 128 sequences live. `board_turn`: every turn board has at least one river board.
All inputs are finite; a program needn't handle non-finite values. No bound on the sum of `hand_live` or of `board_seqs` on one device may be relied on, other than what follows from the above.
Results may differ from a plain program's by a relative error of at most 0.0003.
Values may be sent and summed in bfloat16 or wider, within the bound.
A program may use at most 64 MiB of HBM per device.

v0:
```python
import jax
import jax.numpy as jnp
import numpy as np
from jax import lax
from jax.sharding import PartitionSpec as P

TURNS = 16
KIDS = 8


def hand_cards(count):
    card_pairs = [
        (lower_card, upper_card)
        for lower_card in range(52)
        for upper_card in range(lower_card + 1, 52)
    ]
    table = np.array(card_pairs[:count], dtype=np.int32)
    return (jnp.asarray(table[:, 0]), jnp.asarray(table[:, 1]))


def apart_table(count):
    first_card, second_card = hand_cards(count)
    return (
        (first_card[:, None] != first_card[None, :])
        & (first_card[:, None] != second_card[None, :])
        & (second_card[:, None] != first_card[None, :])
        & (second_card[:, None] != second_card[None, :])
    )


def payoff_matrix(ranks, live, apart):
    both_live = live[:, None] * live[None, :] > 0
    signs = jnp.sign(ranks[:, None] - ranks[None, :]).astype(jnp.bfloat16)
    return jnp.where(apart & both_live, signs, jnp.bfloat16(0.0))


def children(parent, count_sets, most):
    set_iota = jnp.arange(count_sets, dtype=jnp.int32)
    counts = jnp.sum((parent[None, :] == set_iota[:, None]).astype(jnp.int32), axis=1)
    starts = jnp.cumsum(counts) - counts
    kid_iota = jnp.arange(most, dtype=jnp.int32)
    index = jnp.minimum(starts[:, None] + kid_iota[None, :], parent.shape[0] - 1)
    valid = kid_iota[None, :] < counts[:, None]
    return (index, valid)


def segment_best(values, index, valid):
    picked = values[index]
    shape = valid.shape + (1,) * (values.ndim - 1)
    return jnp.max(jnp.where(valid.reshape(shape), picked, -jnp.inf), axis=1)


def local(reach, stake, hand_rank, hand_live, board_seqs, board_turn, seq_parent, set_parent):
    moved = lax.all_to_all(reach, ("grp", "dev"), split_axis=1, concat_axis=0, tiled=True)
    total_seqs = moved.shape[0]
    local_boards = moved.shape[1]
    hands = moved.shape[2]
    river_sets = set_parent.shape[0]
    apart = apart_table(hands)
    kid_index, kid_valid = children(seq_parent, river_sets, KIDS)
    seq_iota = jnp.arange(total_seqs, dtype=jnp.int32)
    river_list = []
    for board in range(local_boards):
        live_rows = (seq_iota < board_seqs[board]).astype(jnp.bfloat16)
        rows = moved[:, board, :] * live_rows[:, None]
        matrix = payoff_matrix(hand_rank[board], hand_live[board], apart)
        product = lax.dot_general(
            rows, matrix, (((1,), (1,)), ((), ())), preferred_element_type=jnp.float32
        )
        leaf = product * stake[:, None]
        river_list.append(segment_best(leaf, kid_index, kid_valid))
    river = jnp.stack(river_list, axis=1)
    turn_iota = jnp.arange(TURNS, dtype=jnp.int32)
    devices = lax.axis_size(("grp", "dev"))
    owned_sets = river_sets // devices
    owned = lax.all_to_all(river, ("grp", "dev"), split_axis=0, concat_axis=1, tiled=True)
    onehot = (board_turn[:, 0][None, :] == turn_iota[:, None]).astype(jnp.float32)
    chance = jnp.einsum("tb,pbh->pth", onehot, owned, precision=lax.Precision.HIGHEST)
    set_count = river_sets // 4
    set_iota = jnp.arange(set_count, dtype=jnp.int32)
    first_set = lax.axis_index(("grp", "dev")) * owned_sets
    parent_set = set_parent[first_set + 0]
    chosen = (set_iota == parent_set)[:, None, None]
    candidate = jnp.where(chosen, chance[0][None], -jnp.inf)
    best = lax.pmax(candidate, ("grp", "dev"))
    return (river, best)


def solution(mesh):
    in_specs = (
        P(("grp", "dev"), None, None),
        P(),
        P(("grp", "dev"), None),
        P(("grp", "dev"), None),
        P(("grp", "dev")),
        P(),
        P(),
        P(),
    )
    out_specs = (P(None, ("grp", "dev"), None), P())
    return jax.shard_map(local, mesh=mesh, in_specs=in_specs, out_specs=out_specs, check_vma=False)
```

profile of v0, /device:TPU:0, one launch (start us, length us, event | category | flops | bytes accessed | tf_op | source)
XLA Modules:
  0.0 209.9 jit_solution(5315465424213060597)
XLA Ops:
  7.2 2.5 %copy.39 = bf16[4,64,1326]{2,0,1:T(4,128)(2,1)} copy(bf16[4,64,1326]{2,1,0:T(8,128)(2,1)} %param.10) | data formatting | bytes 1357824 | tf_op args[0]
  9.8 7.3 %all-to-all-start = ((bf16[4,64,1326]{2,0,1:T(4,128)(2,1)}), bf16[4,64,1326]{2,0,1:T(4,128)(2,1)S(1)}, u32[]{:S(2)}, u32[]{:S(2)}) async-start(bf16[4,64,1326]{2,0,1:T(4,128)(2,1)} %copy.39), calls=%async_computation | async-start | bytes 1441792 | tf_op jit(solution)/shard_map/all_to_all | solution.py:54
  17.1 0.1 convert_reduce_fusion
  17.2 0.1 copy.42
  17.3 0.1 reduce.2
  17.5 0.1 compare_select_fusion
  17.5 0.1 reshape.133
  17.6 0.6 fusion.26
  18.2 0.6 compare_convert_fusion
  18.9 0.7 compare_convert_fusion.1
  19.8 17.9 %all-to-all-done = bf16[4,64,1326]{2,0,1:T(4,128)(2,1)S(1)} async-done(((bf16[4,64,1326]{2,0,1:T(4,128)(2,1)}), bf16[4,64,1326]{2,0,1:T(4,128)(2,1)S(1)}, u32[]{:S(2)}, u32[]{:S(2)}) %all-to-all-start) | async-done | bytes 678944 | tf_op jit(solution)/shard_map/all_to_all | solution.py:54
  37.6 0.6 copy.40
  38.2 1.0 fusion.25
  39.2 1.0 copy.44
  40.2 4.6 %fusion.11 = f32[128,1326]{0,1:T(8,128)S(1)} fusion(s32[1326]{0:T(1024)S(1)} %get-tuple-element.13, s32[1326]{0:T(1024)S(1)} %get-tuple-element.20, s32[1326]{0:T(1024)S(1)} %copy-done.8, s32[1326]{0:T(1024)S(1)} %copy-done.7, bf16[128,1,1326]{0,2,1:T(8,128)(2,1)S(1)} %copy.44, f32[128]{0:T(128)S(1)} %copy-done.5, bf16[128]{0:T(256)(128)(2,1)S(1)} %compare_convert_fusion), kind=kOutput, calls=%fused_computation.14 | convolution fusion | flops 475073984 | bytes 1040352 | tf_op jit(solution)/shard_map/dot_general | solution.py:67
  44.9 0.3 copy.45
  45.1 1.2 copy.41
  46.3 4.6 %fusion.8 = f32[128,1326]{0,1:T(8,128)S(1)} fusion(s32[1326]{0:T(1024)S(1)} %get-tuple-element.12, s32[1326]{0:T(1024)S(1)} %get-tuple-element.21, s32[1326]{0:T(1024)S(1)} %copy-done.8, s32[1326]{0:T(1024)S(1)} %copy-done.7, bf16[128,1,1326]{0,2,1:T(8,128)(2,1)S(1)} %copy.41, f32[128]{0:T(128)S(1)} %copy-done.5, bf16[128]{0:T(256)(128)(2,1)S(1)} %compare_convert_fusion.1), kind=kOutput, calls=%fused_computation.13 | convolution fusion | flops 475073984 | bytes 1040352 | tf_op jit(solution)/shard_map/dot_general | solution.py:67
  50.9 0.3 copy.43
  51.2 1.2 gather_fusion.1
  52.5 2.3 %gather_fusion = f32[256,1326]{1,0:T(8,128)} fusion(f32[128,1326]{1,0:T(8,128)S(1)} %copy.43, s32[1024]{0:T(1024)S(1)} %pad_clamp_fusion), kind=kCustom, calls=%fused_computation | custom fusion | bytes 2716672 | tf_op jit(solution)/shard_map/gather | solution.py:48
  54.8 2.3 %fusion.17 = (f32[32,1326]{1,0:T(8,128)S(1)}, f32[32,1326]{1,0:T(8,128)S(1)}) fusion(f32[256,1326]{1,0:T(8,128)} %gather_fusion, pred[32,8]{1,0:T(8,128)(4,1)S(1)} %iota_compare_fusion.1, f32[256,1326]{1,0:T(8,128)S(1)} %gather_fusion.1), kind=kLoop, calls=%fused_computation.21 | loop fusion | flops 1272960 | bytes 3055360 | tf_op jit(solution)/shard_map/reduce_max | solution.py:50
  57.1 1.0 copy.47
  58.2 2.6 %all-to-all-start.1 = ((f32[32,2,1326]{2,1,0:T(2,128)}), f32[32,2,1326]{2,1,0:T(2,128)S(1)}, u32[]{:S(2)}, u32[]{:S(2)}) async-start(f32[32,2,1326]{2,1,0:T(2,128)} %copy.47), calls=%async_computation.1 | async-start | bytes 720896 | tf_op jit(solution)/shard_map/all_to_all | solution.py:76
  60.8 0.6 dynamic_slice.3
  61.4 0.6 iota_compare_fusion.4
  62.1 11.5 %all-to-all-done.1 = f32[32,2,1326]{2,1,0:T(2,128)S(1)} async-done(((f32[32,2,1326]{2,1,0:T(2,128)}), f32[32,2,1326]{2,1,0:T(2,128)S(1)}, u32[]{:S(2)}, u32[]{:S(2)}) %all-to-all-start.1) | async-done | bytes 339488 | tf_op jit(solution)/shard_map/all_to_all | solution.py:76
  73.6 0.2 reshape.130
  73.9 0.2 convolution_bitcast_fusion
  74.1 1.0 broadcast_select_fusion
  75.1 125.9 %all-reduce.2.cloned.1.call-done = f32[8,16,1326]{2,1,0:T(8,128)} async-done(((f32[8,16,1326]{2,1,0:T(8,128)}), f32[8,16,1326]{2,1,0:T(8,128)}) %all-reduce.2.cloned.1.call-update) | async-done | bytes 678928 | tf_op jit(solution)/shard_map/pmax | solution.py:85
  201.0 2.0 copy.49
  (26 shorter events, 0.3 us)
Async XLA Ops:
  7.2 9.9 %copy-start.4 = (s32[128]{0:T(128)S(1)}, s32[128]{0:T(128)}, u32[]{:S(2)}) copy-start(s32[128]{0:T(128)} %param.16) | copy-start | bytes 1540
  7.2 10.5 %copy-start.2 = (s32[2]{0:T(128)S(1)}, s32[2]{0:T(128)}, u32[]{:S(2)}) copy-start(s32[2]{0:T(128)} %param.14) | copy-start | bytes 28
  7.2 12.4 %copy-start = (s32[2,1326]{1,0:T(2,128)S(1)}, s32[2,1326]{1,0:T(2,128)}, u32[]{:S(2)}) copy-start(s32[2,1326]{1,0:T(2,128)} %param.12) | copy-start | bytes 31828
  7.2 12.4 %copy-start.1 = (s32[2,1326]{1,0:T(2,128)S(1)}, s32[2,1326]{1,0:T(2,128)}, u32[]{:S(2)}) copy-start(s32[2,1326]{1,0:T(2,128)} %param.13) | copy-start | bytes 31828
  9.8 27.9 %all-to-all-start = ((bf16[4,64,1326]{2,0,1:T(4,128)(2,1)}), bf16[4,64,1326]{2,0,1:T(4,128)(2,1)S(1)}, u32[]{:S(2)}, u32[]{:S(2)}) async-start(bf16[4,64,1326]{2,0,1:T(4,128)(2,1)} %copy.39), calls=%async_computation | async-start | bytes 1441792 | tf_op jit(solution)/shard_map/all_to_all | solution.py:54
  38.2 2.0 copy-start.5
  38.2 2.0 copy-start.7
  38.2 2.0 copy-start.8
  57.1 3.7 %copy-start.6 = (s32[32]{0:T(128)S(1)}, s32[32]{0:T(128)}, u32[]{:S(2)}) copy-start(s32[32]{0:T(128)} %param.17) | copy-start | bytes 388
  57.1 16.8 %copy-start.3 = (s32[64,1]{0,1:T(1,128)S(1)}, s32[64,1]{0,1:T(1,128)}, u32[]{:S(2)}) copy-start(s32[64,1]{0,1:T(1,128)} %param.15) | copy-start | bytes 772
  58.2 15.4 %all-to-all-start.1 = ((f32[32,2,1326]{2,1,0:T(2,128)}), f32[32,2,1326]{2,1,0:T(2,128)S(1)}, u32[]{:S(2)}, u32[]{:S(2)}) async-start(f32[32,2,1326]{2,1,0:T(2,128)} %copy.47), calls=%async_computation.1 | async-start | bytes 720896 | tf_op jit(solution)/shard_map/all_to_all | solution.py:76
  60.8 140.3 %all-reduce.2.cloned.1.call-start = ((), (), s32[]{:S(2)}) async-start(), calls=%async_computation.2 | async-start | bytes 1441792 | tf_op jit(solution)/shard_map/pmax | solution.py:85
Sparse Core Ops, SparseCore 0:
  75.2 125.7 all-reduce.1
where the time goes:
time: 210 us
  waiting for transfers between devices  155 us (74%)
  local copies, waits for them, and re-layouts  15.1 us (7%)
  between operations  14.3 us (7%)
  starting transfers between devices  9.93 us (5%)
  matrix products  9.5 us (5%)
  other arithmetic  5.76 us (3%)
    pmax x1, waiting for transfers between devices, local(): best = lax.pmax(candidate, ('grp', 'dev'))  126 us
    all_to_all x1, waiting for transfers between devices, local(): lax.all_to_all(reach, ('grp', 'dev'), split_axis=1, concat_axis=0, tiled=...  17.9 us
    all_to_all x1, waiting for transfers between devices, local(): lax.all_to_all(river, ('grp', 'dev'), split_axis=0, concat_axis=1, tiled=...  11.5 us
    dot_general x2, matrix products, local(): lax.dot_general(rows, matrix, (((1,), (1,)), ((), ())), preferred_element...  9.25 us
    all_to_all x1, starting transfers between devices, local(): lax.all_to_all(reach, ('grp', 'dev'), split_axis=1, concat_axis=0, tiled=...  7.3 us
    unnamed x21, local copies, waits for them, and re-layouts  5.63 us
  transfers between devices with their start and end apart: 3, of which 3 were waited for; matrix products, arithmetic and copies ran while one was open for 2% of the time, Pallas kernels for 0%

commit v1 on v0

--- a/solution.py
+++ b/solution.py
@@ -51,7 +51,15 @@
 
 
 def local(reach, stake, hand_rank, hand_live, board_seqs, board_turn, seq_parent, set_parent):
-    moved = lax.all_to_all(reach, ("grp", "dev"), split_axis=1, concat_axis=0, tiled=True)
+    moved = jnp.concatenate(
+        lax.all_to_all(
+            jnp.stack(jnp.split(reach, lax.axis_size(("grp", "dev")), axis=1)),
+            axis_name=("grp", "dev"),
+            split_axis=0,
+            concat_axis=0,
+        ),
+        axis=0,
+    )
     total_seqs = moved.shape[0]
     local_boards = moved.shape[1]
     hands = moved.shape[2]

time: 210 us -> 257 us (1.22)
  local copies, waits for them, and re-layouts: 15.1 us -> 60.6 us
    unnamed x21 -> x51, local copies, waits for them, and re-layouts: 5.63 us -> 50.2 us
where the time goes in v1:
time: 257 us; the launch traced here: 255 us
  waiting for transfers between devices  155 us (60%)
  local copies, waits for them, and re-layouts  60.6 us (24%)
  between operations  14.3 us (6%)
  starting transfers between devices  9.93 us (4%)
  matrix products  9.48 us (4%)
  other arithmetic  5.76 us (2%)
    pmax x1, waiting for transfers between devices, local(): best = lax.pmax(candidate, ('grp', 'dev'))  126 us
    unnamed x51, local copies, waits for them, and re-layouts  50.2 us
    all_to_all x1, waiting for transfers between devices, local(): lax.all_to_all(jnp.stack(jnp.split(reach, lax.axis_size(('grp', 'dev')),...  17.9 us
    all_to_all x1, waiting for transfers between devices, local(): lax.all_to_all(river, ('grp', 'dev'), split_axis=0, concat_axis=1, tiled=...  11.5 us
    dot_general x2, matrix products, local(): lax.dot_general(rows, matrix, (((1,), (1,)), ((), ())), preferred_element...  9.24 us
    all_to_all x1, starting transfers between devices, local(): lax.all_to_all(jnp.stack(jnp.split(reach, lax.axis_size(('grp', 'dev')),...  7.3 us
  transfers between devices with their start and end apart: 3, of which 3 were waited for; matrix products, arithmetic and copies ran while one was open for 2% of the time, Pallas kernels for 0%

profile of v1, /device:TPU:0, one launch (start us, length us, event | category | flops | bytes accessed | tf_op | source)
XLA Modules:
  0.0 255.4 jit_solution(10715277764195847284)
XLA Ops:
  8.7 1.5 constant_dynamic-update-slice_fusion.30
  10.2 1.5 constant_dynamic-update-slice_fusion.29
  11.8 1.5 constant_dynamic-update-slice_fusion.28
  14.8 1.5 constant_dynamic-update-slice_fusion.26
  16.3 1.5 constant_dynamic-update-slice_fusion.25
  17.9 1.5 constant_dynamic-update-slice_fusion.24
  20.9 1.5 constant_dynamic-update-slice_fusion.22
  22.4 1.5 constant_dynamic-update-slice_fusion.21
  27.0 1.5 constant_dynamic-update-slice_fusion.18
  28.5 1.5 constant_dynamic-update-slice_fusion.17
  30.0 1.5 constant_dynamic-update-slice_fusion.16
  33.0 1.5 constant_dynamic-update-slice_fusion.14
  34.6 1.5 constant_dynamic-update-slice_fusion.13
  36.1 1.5 constant_dynamic-update-slice_fusion.12
  39.1 1.5 constant_dynamic-update-slice_fusion.10
  40.6 1.5 constant_dynamic-update-slice_fusion.9
  42.2 1.5 constant_dynamic-update-slice_fusion.8
  45.2 1.5 constant_dynamic-update-slice_fusion.6
  46.7 1.5 constant_dynamic-update-slice_fusion.5
  48.2 1.5 constant_dynamic-update-slice_fusion.4
  52.8 1.5 constant_dynamic-update-slice_fusion.1
  54.3 1.5 constant_dynamic-update-slice_fusion
  55.8 7.3 %all-to-all-start = ((bf16[32,4,2,1326]{3,2,1,0:T(2,128)(2,1)}), bf16[32,4,2,1326]{3,2,1,0:T(2,128)(2,1)S(1)}, u32[]{:S(2)}, u32[]{:S(2)}) async-start(bf16[32,4,2,1326]{3,2,1,0:T(2,128)(2,1)} %constant_dynamic-update-slice_fusion), calls=%async_computation | async-start | bytes 1441792 | tf_op jit(solution)/shard_map/all_to_all | solution.py:55
  65.9 17.9 %all-to-all-done = bf16[32,4,2,1326]{3,2,1,0:T(2,128)(2,1)S(1)} async-done(((bf16[32,4,2,1326]{3,2,1,0:T(2,128)(2,1)}), bf16[32,4,2,1326]{3,2,1,0:T(2,128)(2,1)S(1)}, u32[]{:S(2)}, u32[]{:S(2)}) %all-to-all-start) | async-done | bytes 678944 | tf_op jit(solution)/shard_map/all_to_all | solution.py:55
  85.7 4.6 %fusion.11 = f32[128,1326]{0,1:T(8,128)S(1)} fusion(s32[1326]{0:T(1024)S(1)} %get-tuple-element.13, s32[1326]{0:T(1024)S(1)} %get-tuple-element.20, s32[1326]{0:T(1024)S(1)} %copy-done.8, s32[1326]{0:T(1024)S(1)} %copy-done.7, bf16[128,1,1326]{0,2,1:T(8,128)(2,1)S(1)} %copy.37, f32[128]{0:T(128)S(1)} %copy-done.5, bf16[128]{0:T(256)(128)(2,1)S(1)} %compare_convert_fusion), kind=kOutput, calls=%fused_computation.14 | convolution fusion | flops 475073984 | bytes 1040352 | tf_op jit(solution)/shard_map/dot_general | solution.py:75
  91.8 4.6 %fusion.8 = f32[128,1326]{0,1:T(8,128)S(1)} fusion(s32[1326]{0:T(1024)S(1)} %get-tuple-element.12, s32[1326]{0:T(1024)S(1)} %get-tuple-element.21, s32[1326]{0:T(1024)S(1)} %copy-done.8, s32[1326]{0:T(1024)S(1)} %copy-done.7, bf16[128,1,1326]{0,2,1:T(8,128)(2,1)S(1)} %copy.34, f32[128]{0:T(128)S(1)} %copy-done.5, bf16[128]{0:T(256)(128)(2,1)S(1)} %compare_convert_fusion.1), kind=kOutput, calls=%fused_computation.13 | convolution fusion | flops 475073984 | bytes 1040352 | tf_op jit(solution)/shard_map/dot_general | solution.py:75
  97.9 2.3 gather_fusion
  100.2 2.3 fusion.17
  103.6 2.6 %all-to-all-start.1 = ((f32[32,2,1326]{2,1,0:T(2,128)}), f32[32,2,1326]{2,1,0:T(2,128)S(1)}, u32[]{:S(2)}, u32[]{:S(2)}) async-start(f32[32,2,1326]{2,1,0:T(2,128)} %copy.40), calls=%async_computation.1 | async-start | bytes 720896 | tf_op jit(solution)/shard_map/all_to_all | solution.py:84
  107.5 11.5 %all-to-all-done.1 = f32[32,2,1326]{2,1,0:T(2,128)S(1)} async-done(((f32[32,2,1326]{2,1,0:T(2,128)}), f32[32,2,1326]{2,1,0:T(2,128)S(1)}, u32[]{:S(2)}, u32[]{:S(2)}) %all-to-all-start.1) | async-done | bytes 339488 | tf_op jit(solution)/shard_map/all_to_all | solution.py:84
  120.6 125.9 %all-reduce.2.cloned.1.call-done = f32[8,16,1326]{2,1,0:T(8,128)} async-done(((f32[8,16,1326]{2,1,0:T(8,128)}), f32[8,16,1326]{2,1,0:T(8,128)}) %all-reduce.2.cloned.1.call-update) | async-done | bytes 678928 | tf_op jit(solution)/shard_map/pmax | solution.py:93
  246.5 2.0 copy.73
  (56 shorter events, 26.5 us)
Async XLA Ops:
  7.2 56.0 %copy-start.4 = (s32[128]{0:T(128)S(1)}, s32[128]{0:T(128)}, u32[]{:S(2)}) copy-start(s32[128]{0:T(128)} %param.16) | copy-start | bytes 1540
  10.2 53.5 %copy-start.2 = (s32[2]{0:T(128)S(1)}, s32[2]{0:T(128)}, u32[]{:S(2)}) copy-start(s32[2]{0:T(128)} %param.14) | copy-start | bytes 28
  11.7 53.9 %copy-start = (s32[2,1326]{1,0:T(2,128)S(1)}, s32[2,1326]{1,0:T(2,128)}, u32[]{:S(2)}) copy-start(s32[2,1326]{1,0:T(2,128)} %param.12) | copy-start | bytes 31828
  11.8 54.0 %copy-start.1 = (s32[2,1326]{1,0:T(2,128)S(1)}, s32[2,1326]{1,0:T(2,128)}, u32[]{:S(2)}) copy-start(s32[2,1326]{1,0:T(2,128)} %param.13) | copy-start | bytes 31828
  55.8 27.9 %all-to-all-start = ((bf16[32,4,2,1326]{3,2,1,0:T(2,128)(2,1)}), bf16[32,4,2,1326]{3,2,1,0:T(2,128)(2,1)S(1)}, u32[]{:S(2)}, u32[]{:S(2)}) async-start(bf16[32,4,2,1326]{3,2,1,0:T(2,128)(2,1)} %constant_dynamic-update-slice_fusion), calls=%async_computation | async-start | bytes 1441792 | tf_op jit(solution)/shard_map/all_to_all | solution.py:55
  83.7 2.0 copy-start.5
  83.7 2.0 copy-start.7
  83.7 2.0 copy-start.8
  102.6 3.7 %copy-start.6 = (s32[32]{0:T(128)S(1)}, s32[32]{0:T(128)}, u32[]{:S(2)}) copy-start(s32[32]{0:T(128)} %param.17) | copy-start | bytes 388
  102.6 16.8 %copy-start.3 = (s32[64,1]{0,1:T(1,128)S(1)}, s32[64,1]{0,1:T(1,128)}, u32[]{:S(2)}) copy-start(s32[64,1]{0,1:T(1,128)} %param.15) | copy-start | bytes 772
  103.6 15.4 %all-to-all-start.1 = ((f32[32,2,1326]{2,1,0:T(2,128)}), f32[32,2,1326]{2,1,0:T(2,128)S(1)}, u32[]{:S(2)}, u32[]{:S(2)}) async-start(f32[32,2,1326]{2,1,0:T(2,128)} %copy.40), calls=%async_computation.1 | async-start | bytes 720896 | tf_op jit(solution)/shard_map/all_to_all | solution.py:84
  106.2 140.3 %all-reduce.2.cloned.1.call-start = ((), (), s32[]{:S(2)}) async-start(), calls=%async_computation.2 | async-start | bytes 1441792 | tf_op jit(solution)/shard_map/pmax | solution.py:93
Sparse Core Ops, SparseCore 0:
  120.7 125.7 all-reduce.1
